TPU v7x, 512 devices: a whole 4x4x16 slice. The times are simulated.
512 devices in a mesh: gx: 32 (over z, core), gy: 4 (over x), gz: 4 (over y).
Axes of the slice: x: 4, y: 4, z: 16, core: 2. Of those that a mesh axis runs over, the one named last changes fastest.
Arguments:
- source_field: float32 [3, 256, 32, 512], P(None, 'gx', 'gy', 'gz'), may hold values from -6 to 6
- cell_contrast: bfloat16 [65536, 1536], P(('gx', 'gy', 'gz')), may hold values from 0.19921875 to 2
- point_field: bfloat16 [3, 65536], P(None, ('gx', 'gy', 'gz')), may hold values from -3 to 3
- point_class: int32 [65536, 1], P(('gx', 'gy', 'gz')), may hold values from 0 to 31; in each aligned block of 128 rows (0 to 127, 128 to 255, ...) at most 8 rows name the same one
- cell_kind: int32 [65536], P(('gx', 'gy', 'gz')), may hold values from 0 to 3
- inverse_blocks: float32 [32, 4, 3, 3, 512], P('gx'), may hold values from -0.3 to 0.3
Outputs:
- newton_step: float32 [3, 256, 32, 512], P(None, 'gx', 'gy', 'gz')
- krylov_residual: float32 [3, 256, 32, 512], P(None, 'gx', 'gy', 'gz')
Inputs may be any that keep to these rules, and one draw needn't show every extreme that they name: `point_class`: among the 128 points of one device's block no class is named more than 8 times, a bound that some block reaches there.
All inputs are finite; a program needn't handle non-finite values.
Results may differ from a plain program's by a relative error of at most 0.0076.
Values may be sent and summed in bfloat16 or wider, within the bound.
A program may use at most 64 MiB of HBM per device.

v0:
```python
import math
import jax
import jax.numpy as jnp
from jax import lax
from jax.sharding import PartitionSpec as P

CELL = 8
VOX = 512
TYPES = 4
ZP = 8
ITERS = 3
kerr_scale = 0.1


def with_halo(block, sides, width):
    for axis, dim in sides:
        count = lax.axis_size(axis)
        forward = [(i, i + 1) for i in range(count - 1)]
        backward = [(target, source) for source, target in forward]
        low = lax.ppermute(
            lax.slice_in_dim(block, block.shape[dim] - width, None, axis=dim), axis, forward
        )
        high = lax.ppermute(lax.slice_in_dim(block, 0, width, axis=dim), axis, backward)
        block = jnp.concatenate([low, block, high], axis=dim)
    return block


def hartley_table():
    voxel_index = jnp.arange(VOX, dtype=jnp.int32)
    along_one = voxel_index // (CELL * CELL)
    along_two = voxel_index // CELL % CELL
    along_three = voxel_index % CELL
    phase_index = (
        along_one[:, None] * along_one[None, :]
        + along_two[:, None] * along_two[None, :]
        + along_three[:, None] * along_three[None, :]
    ) % CELL
    phase_angle = 2.0 * math.pi / CELL * phase_index.astype(jnp.float32)
    return ((jnp.cos(phase_angle) + jnp.sin(phase_angle)) / math.sqrt(VOX)).astype(jnp.bfloat16)


def cell_solve(contrast, point_values, blocks, hartley):
    row_count = contrast.shape[0]
    weights = contrast.reshape(row_count, 3, VOX).astype(jnp.float32)
    base_field = point_values.astype(jnp.float32)[:, :, None]

    def correction(polarization):
        spectrum = jnp.dot(
            polarization.reshape(row_count * 3, VOX), hartley, preferred_element_type=jnp.float32
        ).reshape(row_count, 3, VOX)
        mixed_spectrum = jnp.sum(blocks * spectrum[:, None, :, :], axis=2).astype(jnp.bfloat16)
        return jnp.dot(
            mixed_spectrum.reshape(row_count * 3, VOX), hartley, preferred_element_type=jnp.float32
        ).reshape(row_count, 3, VOX)

    local_field = base_field - correction((weights * base_field).astype(jnp.bfloat16))
    kerr_polar = (weights * local_field * (1.0 + kerr_scale * local_field * local_field)).astype(
        jnp.bfloat16
    )
    final_field = base_field - correction(kerr_polar)
    flux_mean = jnp.mean((1.0 + weights) * final_field, axis=2)
    stiffness = 0.5 + jnp.mean(weights * final_field * final_field, axis=(1, 2))
    return jnp.concatenate([flux_mean, stiffness[:, None]], axis=1)


def solve_batched(contrast, point_values, keys, library, hartley):
    return cell_solve(contrast, point_values, library[keys], hartley)


def operate(field, diagonal):
    padded = with_halo(field, (("gx", 1), ("gy", 2), ("gz", 3)), 1)
    beside = padded[:, 2:, 1:-1, 1:-1] + padded[:, :-2, 1:-1, 1:-1]
    beside = beside + padded[:, 1:-1, 2:, 1:-1] + padded[:, 1:-1, :-2, 1:-1]
    beside = beside + padded[:, 1:-1, 1:-1, 2:] + padded[:, 1:-1, 1:-1, :-2]
    return (6.0 + diagonal)[None] * field - beside


def squares(residual):
    return lax.psum(jnp.sum(residual * residual), ("gx", "gy", "gz"))


def per_device(source_field, cell_contrast, point_field, point_class, cell_kind, inverse_blocks):
    hartley = hartley_table()
    point_values = point_field.T
    library = lax.all_gather(inverse_blocks, "gx", axis=0, tiled=True)
    library = library.reshape(library.shape[0] * library.shape[1], 3, 3, VOX)
    chosen = point_class[:, 0] * TYPES + cell_kind
    summary = solve_batched(cell_contrast, point_values, chosen, library, hartley)
    extent_x = source_field.shape[1]
    extent_y = source_field.shape[2]
    extent_z = source_field.shape[3]
    blocks_z = extent_z // ZP
    stiffness_grid = jnp.broadcast_to(
        summary[:, 3].reshape(1, extent_y, blocks_z, 1), (extent_x, extent_y, blocks_z, ZP)
    ).reshape(extent_x, extent_y, extent_z)
    flux_grid = jnp.broadcast_to(
        summary[:, :3].T.reshape(3, 1, extent_y, blocks_z, 1), (3, extent_x, extent_y, blocks_z, ZP)
    ).reshape(3, extent_x, extent_y, extent_z)
    right = source_field - flux_grid
    newton_step = jnp.zeros_like(right)
    residual = right
    direction = right
    norm_now = squares(residual)
    for iteration in range(ITERS):
        image = operate(direction, stiffness_grid)
        alpha = norm_now / lax.psum(jnp.sum(direction * image), ("gx", "gy", "gz"))
        newton_step = newton_step + alpha * direction
        residual = residual - alpha * image
        norm_next = squares(residual)
        direction = residual + norm_next / norm_now * direction
        norm_now = norm_next
    return (newton_step, residual)


def solution(mesh):
    placed = (
        P(None, "gx", "gy", "gz"),
        P(("gx", "gy", "gz"), None),
        P(None, ("gx", "gy", "gz")),
        P(("gx", "gy", "gz"), None),
        P(("gx", "gy", "gz")),
        P("gx", None, None, None, None),
    )
    return jax.shard_map(
        per_device,
        mesh=mesh,
        in_specs=placed,
        out_specs=(P(None, "gx", "gy", "gz"), P(None, "gx", "gy", "gz")),
        check_vma=False,
    )
```

profile of v0, /device:TPU:1, one launch (start us, length us, event | category | flops | bytes accessed | tf_op | source)
XLA Modules:
  0.0 722.5 jit_solution(11703445166906747007)
XLA Ops:
  7.2 0.7 all-gather.2.cloned.1.call-update
  7.9 1.2 copy.34
  9.1 0.2 copy.35
  9.3 0.7 convert_bitcast_fusion
  10.1 4.7 fusion.12
  14.8 1.5 copy.39
  16.4 71.8 %all-gather.2.cloned.1.call-done = f32[32,4,3,3,512]{4,1,3,2,0:T(4,128)} async-done(((f32[1,4,3,3,512]{4,1,3,2,0:T(4,128)}), f32[32,4,3,3,512]{4,1,3,2,0:T(4,128)}) %all-gather.2.cloned.1.call-update) | async-done | bytes 2359312 | tf_op jit(solution)/shard_map/all_gather | solution.py:85
  88.2 4.6 copy.45
  92.7 4.3 gather_fusion
  97.1 4.6 multiply_reduce_fusion.1
  101.7 11.6 %fusion.7 = f32[128,3,512]{2,0,1:T(8,128)} fusion(f32[128,3,512]{2,0,1:T(8,128)} %copy-done.1, s32[512]{0:T(512)S(1)} %get-tuple-element.33, s32[512]{0:T(512)S(1)} %get-tuple-element.34, s32[512]{0:T(512)S(1)} %add_select_fusion.4, bf16[128,3,512]{2,1,0:T(4,128)(2,1)} %multiply_reduce_fusion.1, f32[128,3]{0,1:T(4,128)S(1)} %convert_bitcast_fusion), kind=kOutput, calls=%fused_computation.21 | convolution fusion | flops 415039488 | bytes 1973760 | tf_op jit(solution)/shard_map/dot_general | solution.py:48
  113.3 1.7 copy.42
  115.0 3.7 multiply_reduce_fusion
  118.7 4.9 fusion.6
  123.7 0.1 broadcast_in_dim.13
  123.7 0.1 broadcast_in_dim.14
  123.9 0.1 broadcast_in_dim.15
  124.0 2.2 collective-permute-start
  126.2 3.4 collective-permute-start.1
  129.6 0.8 collective-permute-done.1
  130.5 1.3 collective-permute-start.2
  131.8 4.0 collective-permute-start.3
  135.8 0.8 collective-permute-done.3
  136.6 0.1 fusion.70
  136.8 3.1 collective-permute-start.5
  139.9 1.3 collective-permute-start.4
  141.2 0.1 add.216
  141.4 0.1 add.217
  141.5 3.6 collective-permute-done.5
  145.1 3.8 collective-permute-done.4
  148.9 0.8 multiply_reduce_fusion.7
  149.7 102.9 %all-reduce = (f32[]{:T(128)}, f32[]{:T(128)}) all-reduce(f32[]{:T(128)} %get-tuple-element.5, f32[]{:T(128)} %get-tuple-element.4), channel_id=1, replica_groups=mesh['gx'=32,'gy'=4,'gz'=4] {'gx','gy','gz'}, use_global_device_ids=true, to_apply=%region_4.5 | all-reduce | flops 2 | bytes 16 | tf_op jit(solution)/shard_map/psum | solution.py:79
  254.0 0.6 multiply_reduce_fusion.6
  254.6 100.5 %psum.44 = f32[]{:T(128)} all-reduce(f32[]{:T(128)} %multiply_reduce_fusion.6), channel_id=1, replica_groups=mesh['gx'=32,'gy'=4,'gz'=4] {'gx','gy','gz'}, use_global_device_ids=true, to_apply=%region_9.10 | all-reduce | flops 1 | bytes 8 | tf_op jit(solution)/shard_map/psum | solution.py:79
  356.5 2.6 collective-permute-start.6
  359.1 3.0 collective-permute-start.7
  362.1 0.8 collective-permute-done.7
  362.9 1.3 collective-permute-start.8
  364.2 4.0 collective-permute-start.9
  368.2 0.8 collective-permute-done.9
  369.1 0.1 fusion.69
  369.2 2.5 collective-permute-start.11
  371.8 1.3 collective-permute-start.10
  373.1 3.5 collective-permute-done.11
  376.5 3.8 collective-permute-done.10
  380.3 0.8 multiply_reduce_fusion.5
  381.2 101.6 %psum.45 = f32[]{:T(128)} all-reduce(f32[]{:T(128)} %get-tuple-element.12), channel_id=1, replica_groups=mesh['gx'=32,'gy'=4,'gz'=4] {'gx','gy','gz'}, use_global_device_ids=true, to_apply=%region_11.12 | all-reduce | flops 1 | bytes 8 | tf_op jit(solution)/shard_map/psum | solution.py:106
  484.1 0.6 multiply_reduce_fusion.4
  484.8 100.4 %psum.46 = f32[]{:T(128)} all-reduce(f32[]{:T(128)} %get-tuple-element.10), channel_id=1, replica_groups=mesh['gx'=32,'gy'=4,'gz'=4] {'gx','gy','gz'}, use_global_device_ids=true, to_apply=%region_13.14 | all-reduce | flops 1 | bytes 8 | tf_op jit(solution)/shard_map/psum | solution.py:79
  586.5 2.6 collective-permute-start.12
  589.1 3.0 collective-permute-start.13
  592.1 0.8 collective-permute-done.13
  592.9 1.3 collective-permute-start.14
  594.2 4.0 collective-permute-start.15
  598.2 0.8 collective-permute-done.15
  599.1 0.1 fusion.68
  599.2 2.4 collective-permute-start.17
  601.6 1.3 collective-permute-start.16
  602.9 3.5 collective-permute-done.17
  606.4 3.8 collective-permute-done.16
  610.2 0.8 multiply_reduce_fusion.3
  611.0 101.6 %psum.47 = f32[]{:T(128)} all-reduce(f32[]{:T(128)} %get-tuple-element.8), channel_id=1, replica_groups=mesh['gx'=32,'gy'=4,'gz'=4] {'gx','gy','gz'}, use_global_device_ids=true, to_apply=%region_15.16 | all-reduce | flops 1 | bytes 8 | tf_op jit(solution)/shard_map/psum | solution.py:106
  714.0 0.7 multiply_add_fusion
  714.7 0.7 multiply_subtract_fusion
  (36 shorter events, 0.5 us)
Async XLA Ops:
  7.2 81.0 %all-gather.2.cloned.1.call-start = ((), (), s32[]{:S(2)}) async-start(), calls=%async_computation | async-start | bytes 2433024 | tf_op jit(solution)/shard_map/all_gather | solution.py:85
  9.3 5.5 copy-start.1
  10.1 6.3 copy-start.3
  10.1 6.3 copy-start.4
  113.3 5.4 copy-start.2
  118.7 5.3 copy-start
  124.0 5.6 collective-permute-start
  126.2 4.2 collective-permute-start.1
  130.5 5.3 collective-permute-start.2
  131.8 4.8 collective-permute-start.3
  136.8 8.3 %collective-permute-start.5 = (f32[3,10,10,1]{3,2,1,0:T(8,128)S(1)}, f32[3,10,10,1]{3,2,1,0:T(8,128)S(1)}, u32[]{:S(2)}, u32[]{:S(2)}) collective-permute-start(f32[3,10,10,1]{3,2,1,0:T(8,128)S(1)} %get-tuple-element.20), channel_id=1, source_target_pairs={{0,1},{1,2},{2,3},{4,5},{5,6},{6,7},{8,9},{9,10},{10,11},{12,13},{... | collective-permute-start | bytes 3608 | tf_op jit(solution)/shard_map/ppermute | solution.py:20
  139.9 9.0 %collective-permute-start.4 = (f32[3,10,10,1]{3,2,1,0:T(8,128)S(1)}, f32[3,10,10,1]{3,2,1,0:T(8,128)S(1)}, u32[]{:S(2)}, u32[]{:S(2)}) collective-permute-start(f32[3,10,10,1]{3,2,1,0:T(8,128)S(1)} %get-tuple-element.19), channel_id=1, source_target_pairs={{1,0},{2,1},{3,2},{5,4},{6,5},{7,6},{9,8},{10,9},{11,10},{13,12},{... | collective-permute-start | bytes 3608 | tf_op jit(solution)/shard_map/ppermute | solution.py:23
  356.5 5.6 collective-permute-start.6
  359.1 3.8 collective-permute-start.7
  362.9 5.3 collective-permute-start.8
  364.2 4.8 collective-permute-start.9
  369.2 7.3 %collective-permute-start.11 = (f32[3,10,10,1]{3,2,1,0:T(8,128)S(1)}, f32[3,10,10,1]{3,2,1,0:T(8,128)S(1)}, u32[]{:S(2)}, u32[]{:S(2)}) collective-permute-start(f32[3,10,10,1]{3,2,1,0:T(8,128)S(1)} %get-tuple-element.18), channel_id=1, source_target_pairs={{0,1},{1,2},{2,3},{4,5},{5,6},{6,7},{8,9},{9,10},{10,11},{12,13},{... | collective-permute-start | bytes 3608 | tf_op jit(solution)/shard_map/ppermute | solution.py:20
  371.8 8.6 %collective-permute-start.10 = (f32[3,10,10,1]{3,2,1,0:T(8,128)S(1)}, f32[3,10,10,1]{3,2,1,0:T(8,128)S(1)}, u32[]{:S(2)}, u32[]{:S(2)}) collective-permute-start(f32[3,10,10,1]{3,2,1,0:T(8,128)S(1)} %get-tuple-element.17), channel_id=1, source_target_pairs={{1,0},{2,1},{3,2},{5,4},{6,5},{7,6},{9,8},{10,9},{11,10},{13,12},{... | collective-permute-start | bytes 3608 | tf_op jit(solution)/shard_map/ppermute | solution.py:23
  586.5 5.6 collective-permute-start.12
  589.1 3.8 collective-permute-start.13
  592.9 5.3 collective-permute-start.14
  594.2 4.8 collective-permute-start.15
  599.2 7.2 collective-permute-start.17
  601.6 8.6 %collective-permute-start.16 = (f32[3,10,10,1]{3,2,1,0:T(8,128)S(1)}, f32[3,10,10,1]{3,2,1,0:T(8,128)S(1)}, u32[]{:S(2)}, u32[]{:S(2)}) collective-permute-start(f32[3,10,10,1]{3,2,1,0:T(8,128)S(1)} %get-tuple-element.15), channel_id=1, source_target_pairs={{1,0},{2,1},{3,2},{5,4},{6,5},{7,6},{9,8},{10,9},{11,10},{13,12},{... | collective-permute-start | bytes 3608 | tf_op jit(solution)/shard_map/ppermute | solution.py:23
Sparse Core Ops, SparseCore 0:
  10.1 78.0 all-gather.1
where the time goes:
time: 733 us; the launch traced here: 723 us
  blocking collectives  507 us (69%)
  waiting for transfers between devices  99.3 us (14%)
  starting transfers between devices  44.5 us (6%)
  between operations  21.5 us (3%)
  matrix products  21.3 us (3%)
  local copies, waits for them, and re-layouts  14.6 us (2%)
  other arithmetic  14.3 us (2%)
    psum x3, blocking collectives, squares(): return lax.psum(jnp.sum(residual * residual), ('gx', 'gy', 'gz'))  304 us
    psum x2, blocking collectives, per_device(): alpha = norm_now / lax.psum(jnp.sum(direction * image), ('gx', 'gy', 'gz'))  203 us
    all_gather x1, waiting for transfers between devices, per_device(): library = lax.all_gather(inverse_blocks, 'gx', axis=0, tiled=True)  71.8 us
    ppermute x9, starting transfers between devices, with_halo(): lax.ppermute(lax.slice_in_dim(block, block.shape[dim] - width, None, axis...  29.4 us
    dot_general x2, matrix products, correction(): jnp.dot(polarization.reshape(row_count * 3, VOX), hartley, preferred_elem...  16.3 us
    ppermute x9, waiting for transfers between devices, with_halo(): lax.ppermute(lax.slice_in_dim(block, block.shape[dim] - width, None, axis...  15.4 us
    ppermute x9, starting transfers between devices, with_halo(): lax.ppermute(lax.slice_in_dim(block, 0, width, axis=dim), axis, backward)  15.1 us
  transfers between devices with their start and end apart: 19, of which 13 were waited for; matrix products, arithmetic and copies ran while one was open for 1% of the time, Pallas kernels for 0%

commit v1 on v0

--- a/solution.py
+++ b/solution.py
@@ -10,6 +10,11 @@
 ZP = 8
 ITERS = 3
 kerr_scale = 0.1
+
+
+def gather_from_all(shard, axis, dim):
+    copies = jnp.concatenate([shard] * lax.axis_size(axis), axis=dim)
+    return lax.all_to_all(copies, axis, dim, dim, tiled=True)
 
 
 def with_halo(block, sides, width):
@@ -82,7 +87,7 @@
 def per_device(source_field, cell_contrast, point_field, point_class, cell_kind, inverse_blocks):
     hartley = hartley_table()
     point_values = point_field.T
-    library = lax.all_gather(inverse_blocks, "gx", axis=0, tiled=True)
+    library = gather_from_all(inverse_blocks, "gx", 0)
     library = library.reshape(library.shape[0] * library.shape[1], 3, 3, VOX)
     chosen = point_class[:, 0] * TYPES + cell_kind
     summary = solve_batched(cell_contrast, point_values, chosen, library, hartley)

time: 733 us -> 765 us (1.044)
  waiting for transfers between devices: 99.3 us -> 127 us
  starting transfers between devices: 44.5 us -> 64.1 us
  between operations: 21.5 us -> 8.14 us
    all_to_all x0 -> x1, waiting for transfers between devices: none -> 100 us  [gather_from_all(): return lax.all_to_all(copies, axis, dim, dim, tiled=True)]
    all_gather x1 -> x0, waiting for transfers between devices: 71.8 us -> none  [per_device(): library = lax.all_gather(inverse_blocks, 'gx', axis=0, tiled=True)]
    all_to_all x0 -> x1, starting transfers between devices: none -> 16.9 us  [gather_from_all(): return lax.all_to_all(copies, axis, dim, dim, tiled=True)]
where the time goes in v1:
time: 765 us; the launch traced here: 754 us
  blocking collectives  504 us (66%)
  waiting for transfers between devices  127 us (17%)
  starting transfers between devices  64.1 us (8%)
  matrix products  22.4 us (3%)
  local copies, waits for them, and re-layouts  15.4 us (2%)
  other arithmetic  13.6 us (2%)
  between operations  8.14 us (1%)
    psum x3, blocking collectives, squares(): return lax.psum(jnp.sum(residual * residual), ('gx', 'gy', 'gz'))  301 us
    psum x2, blocking collectives, per_device(): alpha = norm_now / lax.psum(jnp.sum(direction * image), ('gx', 'gy', 'gz'))  203 us
    all_to_all x1, waiting for transfers between devices, gather_from_all(): return lax.all_to_all(copies, axis, dim, dim, tiled=True)  100 us
    ppermute x9, starting transfers between devices, with_halo(): lax.ppermute(lax.slice_in_dim(block, block.shape[dim] - width, None, axis...  31.6 us
    dot_general x2, matrix products, correction(): jnp.dot(polarization.reshape(row_count * 3, VOX), hartley, preferred_elem...  17.5 us
    all_to_all x1, starting transfers between devices, gather_from_all(): return lax.all_to_all(copies, axis, dim, dim, tiled=True)  16.9 us
    ppermute x9, starting transfers between devices, with_halo(): lax.ppermute(lax.slice_in_dim(block, 0, width, axis=dim), axis, backward)  15.6 us
  transfers between devices with their start and end apart: 19, of which 13 were waited for; matrix products, arithmetic and copies ran while one was open for 1% of the time, Pallas kernels for 0%

profile of v1, /device:TPU:1, one launch (start us, length us, event | category | flops | bytes accessed | tf_op | source)
XLA Modules:
  0.0 754.4 jit_solution(16817240499726245476)
XLA Ops:
  0.6 2.7 concatenate.78
  3.3 16.9 %all-to-all-start = ((f32[32,4,3,3,512]{4,1,3,2,0:T(4,128)}), f32[32,4,3,3,512]{4,1,3,2,0:T(4,128)S(1)}, u32[]{:S(2)}, u32[]{:S(2)}) async-start(f32[32,4,3,3,512]{4,1,3,2,0:T(4,128)} %concatenate.78), calls=%async_computation | async-start | bytes 4718592 | tf_op jit(solution)/shard_map/all_to_all | solution.py:17
  20.2 0.2 copy.48
  20.4 1.1 copy.49
  21.5 5.9 fusion.12
  27.4 1.5 copy.53
  29.0 100.4 %all-to-all-done = f32[32,4,3,3,512]{4,1,3,2,0:T(4,128)S(1)} async-done(((f32[32,4,3,3,512]{4,1,3,2,0:T(4,128)}), f32[32,4,3,3,512]{4,1,3,2,0:T(4,128)S(1)}, u32[]{:S(2)}, u32[]{:S(2)}) %all-to-all-start) | async-done | bytes 2359328 | tf_op jit(solution)/shard_map/all_to_all | solution.py:17
  129.4 2.9 copy.59
  132.3 4.3 gather_fusion
  136.6 4.6 multiply_reduce_fusion.1
  141.2 11.6 %fusion.7 = f32[128,3,512]{2,0,1:T(8,128)} fusion(f32[128,3,512]{2,0,1:T(8,128)} %copy.49, s32[512]{0:T(512)S(1)} %get-tuple-element.33, s32[512]{0:T(512)S(1)} %get-tuple-element.34, s32[512]{0:T(512)S(1)} %add_select_fusion.4, bf16[128,3,512]{2,1,0:T(4,128)(2,1)} %multiply_reduce_fusion.1, f32[128,3]{0,1:T(4,128)S(1)} %convert_bitcast_fusion), kind=kOutput, calls=%fused_computation.21 | convolution fusion | flops 415039488 | bytes 1973760 | tf_op jit(solution)/shard_map/dot_general | solution.py:53
  152.8 1.7 copy.56
  154.6 3.7 multiply_reduce_fusion
  158.2 4.9 fusion.6
  163.2 0.1 broadcast_in_dim.13
  163.3 0.1 broadcast_in_dim.14
  163.4 0.1 broadcast_in_dim.15
  163.6 2.7 collective-permute-start
  166.3 5.0 collective-permute-start.1
  171.4 0.8 collective-permute-done.1
  172.2 1.3 collective-permute-start.2
  173.5 4.0 collective-permute-start.3
  177.5 0.8 collective-permute-done.3
  178.4 0.1 fusion.70
  178.5 3.2 collective-permute-start.5
  181.7 1.3 collective-permute-start.4
  183.1 0.1 add.216
  183.2 0.1 add.217
  183.3 3.1 collective-permute-done.5
  186.5 4.1 collective-permute-done.4
  190.6 0.8 multiply_reduce_fusion.7
  191.4 102.5 %all-reduce = (f32[]{:T(128)}, f32[]{:T(128)}) all-reduce(f32[]{:T(128)} %get-tuple-element.5, f32[]{:T(128)} %get-tuple-element.4), channel_id=1, replica_groups=mesh['gx'=32,'gy'=4,'gz'=4] {'gx','gy','gz'}, use_global_device_ids=true, to_apply=%region_4.5 | all-reduce | flops 2 | bytes 16 | tf_op jit(solution)/shard_map/psum | solution.py:84
  295.2 0.6 multiply_reduce_fusion.6
  295.8 98.7 %psum.44 = f32[]{:T(128)} all-reduce(f32[]{:T(128)} %multiply_reduce_fusion.6), channel_id=1, replica_groups=mesh['gx'=32,'gy'=4,'gz'=4] {'gx','gy','gz'}, use_global_device_ids=true, to_apply=%region_9.10 | all-reduce | flops 1 | bytes 8 | tf_op jit(solution)/shard_map/psum | solution.py:84
  395.9 2.6 collective-permute-start.6
  398.5 3.5 collective-permute-start.7
  402.0 0.8 collective-permute-done.7
  402.8 1.3 collective-permute-start.8
  404.1 4.0 collective-permute-start.9
  408.2 0.8 collective-permute-done.9
  409.0 0.1 fusion.69
  409.2 2.5 collective-permute-start.11
  411.7 1.3 collective-permute-start.10
  413.0 3.5 collective-permute-done.11
  416.5 3.8 collective-permute-done.10
  420.3 0.8 multiply_reduce_fusion.5
  421.1 101.1 %psum.45 = f32[]{:T(128)} all-reduce(f32[]{:T(128)} %get-tuple-element.12), channel_id=1, replica_groups=mesh['gx'=32,'gy'=4,'gz'=4] {'gx','gy','gz'}, use_global_device_ids=true, to_apply=%region_11.12 | all-reduce | flops 1 | bytes 8 | tf_op jit(solution)/shard_map/psum | solution.py:111
  523.6 0.6 multiply_reduce_fusion.4
  524.2 99.6 %psum.46 = f32[]{:T(128)} all-reduce(f32[]{:T(128)} %get-tuple-element.10), channel_id=1, replica_groups=mesh['gx'=32,'gy'=4,'gz'=4] {'gx','gy','gz'}, use_global_device_ids=true, to_apply=%region_13.14 | all-reduce | flops 1 | bytes 8 | tf_op jit(solution)/shard_map/psum | solution.py:84
  625.2 2.6 collective-permute-start.12
  627.8 3.0 collective-permute-start.13
  630.8 0.8 collective-permute-done.13
  631.6 1.3 collective-permute-start.14
  632.9 4.0 collective-permute-start.15
  636.9 0.8 collective-permute-done.15
  637.8 0.1 fusion.68
  637.9 2.4 collective-permute-start.17
  640.3 1.3 collective-permute-start.16
  641.6 3.5 collective-permute-done.17
  645.1 3.8 collective-permute-done.16
  648.9 0.8 multiply_reduce_fusion.3
  649.7 101.7 %psum.47 = f32[]{:T(128)} all-reduce(f32[]{:T(128)} %get-tuple-element.8), channel_id=1, replica_groups=mesh['gx'=32,'gy'=4,'gz'=4] {'gx','gy','gz'}, use_global_device_ids=true, to_apply=%region_15.16 | all-reduce | flops 1 | bytes 8 | tf_op jit(solution)/shard_map/psum | solution.py:111
  752.7 0.7 multiply_add_fusion
  753.4 0.7 multiply_subtract_fusion
  (38 shorter events, 0.4 us)
Async XLA Ops:
  0.6 19.6 %copy-start.2 = (bf16[128,1536]{1,0:T(8,128)(2,1)S(1)}, bf16[128,1536]{1,0:T(8,128)(2,1)}, u32[]{:S(2)}) copy-start(bf16[128,1536]{1,0:T(8,128)(2,1)} %param.7) | copy-start | bytes 1179652
  3.3 18.2 %copy-start.3 = (bf16[3,128]{1,0:T(4,128)(2,1)S(1)}, bf16[3,128]{1,0:T(4,128)(2,1)}, u32[]{:S(2)}) copy-start(bf16[3,128]{1,0:T(4,128)(2,1)} %param.8) | copy-start | bytes 2308
  3.3 126.1 %all-to-all-start = ((f32[32,4,3,3,512]{4,1,3,2,0:T(4,128)}), f32[32,4,3,3,512]{4,1,3,2,0:T(4,128)S(1)}, u32[]{:S(2)}, u32[]{:S(2)}) async-start(f32[32,4,3,3,512]{4,1,3,2,0:T(4,128)} %concatenate.78), calls=%async_computation | async-start | bytes 4718592 | tf_op jit(solution)/shard_map/all_to_all | solution.py:17
  21.5 7.4 copy-start.4
  21.5 7.4 copy-start.5
  152.8 5.4 copy-start.1
  158.2 5.3 copy-start
  163.6 7.8 %collective-permute-start = (f32[3,1,8,128]{3,2,1,0:T(8,128)S(1)}, f32[3,1,8,128]{3,2,1,0:T(8,128)S(1)}, u32[]{:S(2)}, u32[]{:S(2)}) collective-permute-start(f32[3,1,8,128]{3,2,1,0:T(8,128)S(1)} %get-tuple-element.32), channel_id=1, source_target_pairs={{16,0},{32,16},{48,32},{64,48},{80,64},{96,80},{112,96},{128,112},... | collective-permute-start | bytes 36872 | tf_op jit(solution)/shard_map/ppermute | solution.py:28
  166.3 5.9 collective-permute-start.1
  172.2 5.3 collective-permute-start.2
  173.5 4.8 collective-permute-start.3
  178.5 7.9 %collective-permute-start.5 = (f32[3,10,10,1]{3,2,1,0:T(8,128)S(1)}, f32[3,10,10,1]{3,2,1,0:T(8,128)S(1)}, u32[]{:S(2)}, u32[]{:S(2)}) collective-permute-start(f32[3,10,10,1]{3,2,1,0:T(8,128)S(1)} %get-tuple-element.20), channel_id=1, source_target_pairs={{0,1},{1,2},{2,3},{4,5},{5,6},{6,7},{8,9},{9,10},{10,11},{12,13},{... | collective-permute-start | bytes 3608 | tf_op jit(solution)/shard_map/ppermute | solution.py:25
  181.7 8.8 %collective-permute-start.4 = (f32[3,10,10,1]{3,2,1,0:T(8,128)S(1)}, f32[3,10,10,1]{3,2,1,0:T(8,128)S(1)}, u32[]{:S(2)}, u32[]{:S(2)}) collective-permute-start(f32[3,10,10,1]{3,2,1,0:T(8,128)S(1)} %get-tuple-element.19), channel_id=1, source_target_pairs={{1,0},{2,1},{3,2},{5,4},{6,5},{7,6},{9,8},{10,9},{11,10},{13,12},{... | collective-permute-start | bytes 3608 | tf_op jit(solution)/shard_map/ppermute | solution.py:28
  395.9 6.1 collective-permute-start.6
  398.5 4.3 collective-permute-start.7
  402.8 5.3 collective-permute-start.8
  404.1 4.8 collective-permute-start.9
  409.2 7.3 collective-permute-start.11
  411.7 8.6 %collective-permute-start.10 = (f32[3,10,10,1]{3,2,1,0:T(8,128)S(1)}, f32[3,10,10,1]{3,2,1,0:T(8,128)S(1)}, u32[]{:S(2)}, u32[]{:S(2)}) collective-permute-start(f32[3,10,10,1]{3,2,1,0:T(8,128)S(1)} %get-tuple-element.17), channel_id=1, source_target_pairs={{1,0},{2,1},{3,2},{5,4},{6,5},{7,6},{9,8},{10,9},{11,10},{13,12},{... | collective-permute-start | bytes 3608 | tf_op jit(solution)/shard_map/ppermute | solution.py:28
  625.2 5.6 collective-permute-start.12
  627.8 3.8 collective-permute-start.13
  631.6 5.3 collective-permute-start.14
  632.9 4.8 collective-permute-start.15
  637.9 7.1 collective-permute-start.17
  640.3 8.6 %collective-permute-start.16 = (f32[3,10,10,1]{3,2,1,0:T(8,128)S(1)}, f32[3,10,10,1]{3,2,1,0:T(8,128)S(1)}, u32[]{:S(2)}, u32[]{:S(2)}) collective-permute-start(f32[3,10,10,1]{3,2,1,0:T(8,128)S(1)} %get-tuple-element.15), channel_id=1, source_target_pairs={{1,0},{2,1},{3,2},{5,4},{6,5},{7,6},{9,8},{10,9},{11,10},{13,12},{... | collective-permute-start | bytes 3608 | tf_op jit(solution)/shard_map/ppermute | solution.py:28
